TPU v7x, 32 devices: a whole 2x2x4 slice. The times are simulated.
32 devices in a mesh: seq: 16 (over z, y, core), head: 2 (over x).
Axes of the slice: x: 2, y: 2, z: 4, core: 2. Of those that a mesh axis runs over, the one named last changes fastest.
Arguments:
- tokens: bfloat16 [8192, 5120], P(('seq', 'head')), may hold values from -6 to 6
- w_qkv: bfloat16 [3, 5120, 640], P(None, None, 'head'), may hold values from -0.078125 to 0.078125
- scale_exp: int32 [3, 40, 2], P(None, None, 'head'), may hold values from -2 to 1
- gate_mask: int32 [8192, 2], P('seq', 'head'), may hold values 0 or 1
- rate: float32 [2], P('head'), may hold values from 0.00044194172 to 0.0022097088
- fast_gate: bfloat16 [2, 320, 640], P('head'), may hold values from -0.3125 to 0.3125
- fast_up: bfloat16 [2, 320, 640], P('head'), may hold values from -0.3125 to 0.3125
- fast_down: bfloat16 [2, 320, 640], P('head'), may hold values from -0.25 to 0.25
Outputs:
- answers: bfloat16 [8192, 640], P(('seq', 'head'))
All inputs are finite; a program needn't handle non-finite values. No bound on the sum of `gate_mask` on one device may be relied on, other than what follows from the above.
Results may differ from a plain program's by a relative error of at most 0.012.
Values may be sent and summed in bfloat16 or wider, within the bound.
A program may use at most 64 MiB of HBM per device.

v0:
```python
import jax
import jax.numpy as jnp
from jax import lax
from jax.sharding import PartitionSpec as P


def local_grads(keys, values, weight, old):
    gate = jnp.dot(keys, old[0], preferred_element_type=jnp.float32)
    upper = jnp.dot(keys, old[1], preferred_element_type=jnp.float32)
    sigma = jax.nn.sigmoid(gate)
    active = gate * sigma
    hidden = (active * upper).astype(jnp.bfloat16)
    weighted = (weight[:, None] * values.astype(jnp.float32)).astype(jnp.bfloat16)
    d_hidden = jnp.dot(weighted, old[2], preferred_element_type=jnp.float32)
    d_gate = (d_hidden * upper * sigma * (1.0 + gate * (1.0 - sigma))).astype(jnp.bfloat16)
    d_upper = (d_hidden * active).astype(jnp.bfloat16)
    dims = (((0,), (0,)), ((), ()))
    grad_gate = lax.dot_general(keys, d_gate, dims, preferred_element_type=jnp.float32)
    grad_upper = lax.dot_general(keys, d_upper, dims, preferred_element_type=jnp.float32)
    grad_down = lax.dot_general(weighted, hidden, dims, preferred_element_type=jnp.float32)
    return jnp.stack([grad_gate, grad_upper, grad_down])


def respond(query, renorm):
    gate = jnp.dot(query, renorm[0], preferred_element_type=jnp.float32)
    upper = jnp.dot(query, renorm[1], preferred_element_type=jnp.float32)
    hidden = (jax.nn.silu(gate) * upper).astype(jnp.bfloat16)
    output = lax.dot_general(
        hidden, renorm[2], (((1,), (1,)), ((), ())), preferred_element_type=jnp.float32
    )
    scaled = output * lax.rsqrt(jnp.mean(output * output, axis=-1, keepdims=True) + 1e-05)
    return scaled.astype(jnp.bfloat16)


def body(tokens, w_qkv, scale_exp, gate_mask, rate, fast_gate, fast_up, fast_down):
    factor = jnp.exp2(scale_exp.astype(jnp.float32))[:, :, 0]
    block_rows = w_qkv.shape[1] // factor.shape[1]
    factor = jnp.repeat(factor, block_rows, axis=1)[:, :, None].astype(jnp.bfloat16)
    weff = w_qkv * factor
    triple = jnp.einsum(
        "rd,cdh->rch",
        lax.all_gather(tokens, "head", axis=0, tiled=True),
        weff,
        preferred_element_type=jnp.float32,
    ).astype(jnp.bfloat16)
    query = triple[:, 0]
    keys = triple[:, 1]
    values = triple[:, 2]
    weight = rate[0] * gate_mask[:, 0].astype(jnp.float32)
    old = jnp.stack([fast_gate[0], fast_up[0], fast_down[0]])
    partial_grads = local_grads(keys, values, weight, old)
    old_f = old.astype(jnp.float32)
    old_norm = jnp.sqrt(jnp.sum(old_f * old_f, axis=1))
    total = lax.psum(partial_grads, "seq")
    fresh = old_f + total
    new_sq = jnp.sum(fresh * fresh, axis=1)
    renorm = (fresh * (old_norm / jnp.sqrt(new_sq + 1e-06))[:, None, :]).astype(jnp.bfloat16)
    answer = respond(query, renorm)
    return lax.all_to_all(answer, "head", split_axis=0, concat_axis=1, tiled=True)


def solution(mesh):
    in_specs = (
        P(("seq", "head"), None),
        P(None, None, "head"),
        P(None, None, "head"),
        P("seq", "head"),
        P("head"),
        P("head", None, None),
        P("head", None, None),
        P("head", None, None),
    )
    out_specs = P(("seq", "head"), None)
    return jax.shard_map(body, mesh=mesh, in_specs=in_specs, out_specs=out_specs, check_vma=False)
```

profile of v0, /device:TPU:0, one launch (start us, length us, event | category | flops | bytes accessed | tf_op | source)
XLA Modules:
  0.0 218.8 jit_solution(169645211959964053)
XLA Ops:
  6.5 0.0 copy-start.5
  6.5 0.0 copy-start.4
  6.5 0.0 all-gather.2.cloned.1.call-start
  6.5 0.7 all-gather.2.cloned.1.call-update
  7.3 0.0 all-reduce.2.cloned.1.call-start
  8.0 0.0 copy-done.5
  8.0 0.1 broadcast_bitcast_fusion
  8.1 0.0 copy-done.4
  8.1 72.0 %all-gather.2.cloned.1.call-done = bf16[512,5120]{1,0:T(8,128)(2,1)} async-done(((bf16[256,5120]{1,0:T(8,128)(2,1)}), bf16[512,5120]{1,0:T(8,128)(2,1)}) %all-gather.2.cloned.1.call-update) | async-done | bytes 5242896 | tf_op jit(solution)/shard_map/all_gather | solution.py:42
  80.2 0.0 copy-start.2
  80.2 9.5 %fusion.10 = bf16[512,3,320]{0,2,1:T(8,128)(2,1)S(1)} fusion(bf16[512,5120]{1,0:T(8,128)(2,1)} %all-gather.2.cloned.1.call-done, bf16[3,5120,320]{1,2,0:T(8,128)(2,1)} %param.9, bf16[3,5120]{1,0:T(4,128)(2,1)S(1)} %bitcast.82), kind=kOutput, calls=%fused_computation.12 | convolution fusion | flops 5038571520 | bytes 16087040 | tf_op jit(solution)/shard_map/rd,cdh->rch/dot_general | solution.py:40
  89.7 0.0 copy-done.2
  89.7 0.0 copy-start.1
  89.7 0.6 fusion.23
  90.3 0.4 copy-done.1
  90.7 0.0 copy-start.3
  90.7 0.6 fusion.25
  91.3 0.4 copy-done.3
  91.7 0.6 fusion.27
  92.3 0.6 convolution_bitcast_fusion.1
  92.9 0.8 convolution_bitcast_fusion.2
  93.7 0.6 convolution_bitcast_fusion
  94.3 1.6 pad_maximum_fusion
  95.9 0.0 all-reduce.2.cloned.1.call-update
  96.0 100.3 %all-reduce.2.cloned.1.call-done = f32[3,320,640]{2,1,0:T(8,128)} async-done(((f32[3,320,640]{2,1,0:T(8,128)}), f32[3,320,640]{2,1,0:T(8,128)}) %all-reduce.2.cloned.1.call-update) | async-done | bytes 2457616 | tf_op jit(solution)/shard_map/psum | solution.py:54
  196.2 0.0 copy-start
  196.2 2.4 %fusion.4 = (f32[3,640]{1,0:T(4,128)S(1)}, f32[3,640]{1,0:T(4,128)S(1)}) fusion(bf16[1,320,640]{2,1,0:T(8,128)(2,1)S(1)} %copy-done.3, bf16[1,320,640]{2,1,0:T(8,128)(2,1)S(1)} %copy-done.1, bf16[1,320,640]{2,1,0:T(8,128)(2,1)S(1)} %copy-done.2, f32[3,320,640]{2,1,0:T(8,128)} %all-reduce.2.cloned.1.call-done), kind=kLoop, calls=%fused_computation.6 | loop fusion | flops 4911360 | bytes 3701760 | tf_op jit(solution)/shard_map/reduce_sum | solution.py:53
  198.6 0.1 copy-done
  198.7 0.4 multiply_convert_fusion
  199.0 1.6 fusion.22
  200.7 2.3 %multiply_reduce_fusion.1 = (f32[512]{0:T(512)S(1)}, f32[512,320]{0,1:T(8,128)S(1)}) fusion(bf16[3,320,640]{2,1,0:T(8,128)(2,1)S(1)} %multiply_convert_fusion, f32[512,640]{1,0:T(8,128)} %fusion.22, bf16[512,3,320]{0,2,1:T(8,128)(2,1)S(1)} %fusion.10), kind=kOutput, calls=%fused_computation.30 | convolution fusion | flops 421723648 | bytes 3115008 | tf_op jit(solution)/shard_map/dot_general | solution.py:28
  203.0 0.1 multiply_convert_fusion.6
  203.1 7.9 %all_to_all.19 = bf16[2,256,320]{1,2,0:T(8,128)(2,1)S(1)} all-to-all(bf16[2,256,320]{1,2,0:T(8,128)(2,1)S(1)} %bitcast.79), channel_id=1, replica_groups=mesh['seq'=16,'head'=2] {'head'}, dimensions={0} | all-to-all | bytes 655360 | tf_op jit(solution)/shard_map/all_to_all | solution.py:59
  211.1 0.9 copy.11
  (7 shorter events, 0.1 us)
Async XLA Ops:
  6.5 1.4 copy-start.5
  6.5 1.6 copy-start.4
  6.5 73.6 %all-gather.2.cloned.1.call-start = ((), (), s32[]{:S(2)}) async-start(), calls=%async_computation.1 | async-start | bytes 7864320 | tf_op jit(solution)/shard_map/all_gather | solution.py:42
  7.3 189.0 %all-reduce.2.cloned.1.call-start = ((), (), s32[]{:S(2)}) async-start(), calls=%async_computation.2 | async-start | bytes 4915200 | tf_op jit(solution)/shard_map/psum | solution.py:54
  80.2 9.5 %copy-start.2 = (bf16[1,320,640]{2,1,0:T(8,128)(2,1)S(1)}, bf16[1,320,640]{2,1,0:T(8,128)(2,1)}, u32[]{:S(2)}) copy-start(bf16[1,320,640]{2,1,0:T(8,128)(2,1)} %param.13) | copy-start | bytes 1228804
  89.7 1.0 copy-start.1
  90.7 1.0 copy-start.3
  196.2 2.4 %copy-start = (f32[3,320,640]{2,1,0:T(8,128)S(1)}, f32[3,320,640]{2,1,0:T(8,128)}, u32[]{:S(2)}) copy-start(f32[3,320,640]{2,1,0:T(8,128)} %all-reduce.2.cloned.1.call-done) | copy-start | bytes 7372804
Sparse Core Ops, SparseCore 0:
  8.9 71.2 all-gather.1
  96.1 100.1 all-reduce.1
where the time goes:
time: 219 us
  waiting for transfers between devices  173 us (79%)
  matrix products  17.3 us (8%)
  between operations  14.2 us (6%)
  blocking collectives  7.95 us (4%)
  other arithmetic  4.41 us (2%)
    psum x1, waiting for transfers between devices, body(): total = lax.psum(partial_grads, 'seq')  100 us
    all_gather x1, waiting for transfers between devices, body(): lax.all_gather(tokens, 'head', axis=0, tiled=True)  72 us
    dot_general x1, matrix products, body(): jnp.einsum('rd,cdh->rch', lax.all_gather(tokens, 'head', axis=0, tiled=Tr...  9.51 us
    all_to_all x1, blocking collectives, body(): lax.all_to_all(answer, 'head', split_axis=0, concat_axis=1, tiled=True)  7.95 us
  transfers between devices with their start and end apart: 2, of which 2 were waited for; matrix products, arithmetic and copies ran while one was open for 0% of the time, Pallas kernels for 0%

commit v1 on v0

--- a/solution.py
+++ b/solution.py
@@ -51,7 +51,7 @@
     partial_grads = local_grads(keys, values, weight, old)
     old_f = old.astype(jnp.float32)
     old_norm = jnp.sqrt(jnp.sum(old_f * old_f, axis=1))
-    total = lax.psum(partial_grads, "seq")
+    total = jnp.sum(lax.all_gather(partial_grads, "seq"), axis=0)
     fresh = old_f + total
     new_sq = jnp.sum(fresh * fresh, axis=1)
     renorm = (fresh * (old_norm / jnp.sqrt(new_sq + 1e-06))[:, None, :]).astype(jnp.bfloat16)

time: 219 us -> 330 us (1.51)
  waiting for transfers between devices: 173 us -> 268 us
  other arithmetic: 4.41 us -> 17.5 us
    all_gather x0 -> x1, waiting for transfers between devices: none -> 195 us  [body(): total = jnp.sum(lax.all_gather(partial_grads, 'seq'), axis=0)]
    psum x1 -> x0, waiting for transfers between devices: 100 us -> none  [body(): total = lax.psum(partial_grads, 'seq')]
    reduce_sum x0 -> x1, other arithmetic: none -> 13.9 us  [body(): total = jnp.sum(lax.all_gather(partial_grads, 'seq'), axis=0)]
where the time goes in v1:
time: 330 us; the launch traced here: 329 us
  waiting for transfers between devices  268 us (81%)
  other arithmetic  17.5 us (5%)
  matrix products  17.2 us (5%)
  between operations  14.3 us (4%)
  blocking collectives  8.96 us (3%)
    all_gather x1, waiting for transfers between devices, body(): total = jnp.sum(lax.all_gather(partial_grads, 'seq'), axis=0)  195 us
    all_gather x1, waiting for transfers between devices, body(): lax.all_gather(tokens, 'head', axis=0, tiled=True)  72 us
    reduce_sum x1, other arithmetic, body(): total = jnp.sum(lax.all_gather(partial_grads, 'seq'), axis=0)  13.9 us
    dot_general x1, matrix products, body(): jnp.einsum('rd,cdh->rch', lax.all_gather(tokens, 'head', axis=0, tiled=Tr...  9.51 us
    all_to_all x1, blocking collectives, body(): lax.all_to_all(answer, 'head', split_axis=0, concat_axis=1, tiled=True)  8.96 us
  transfers between devices with their start and end apart: 2, of which 2 were waited for; matrix products, arithmetic and copies ran while one was open for 0% of the time, Pallas kernels for 0%

profile of v1, /device:TPU:0, one launch (start us, length us, event | category | flops | bytes accessed | tf_op | source)
XLA Modules:
  0.0 329.2 jit_solution(3879309964370882839)
XLA Ops:
  6.5 0.0 copy-start.7
  6.5 0.0 copy-start.6
  6.5 0.0 all-gather.4.cloned.1.call-start
  6.5 0.7 all-gather.4.cloned.1.call-update
  7.3 0.0 all-gather.6.cloned.1.call-start
  8.0 0.0 copy-done.7
  8.0 0.1 broadcast_bitcast_fusion
  8.1 0.0 copy-done.6
  8.1 72.0 %all-gather.4.cloned.1.call-done = bf16[512,5120]{1,0:T(8,128)(2,1)} async-done(((bf16[256,5120]{1,0:T(8,128)(2,1)}), bf16[512,5120]{1,0:T(8,128)(2,1)}) %all-gather.4.cloned.1.call-update) | async-done | bytes 5242896 | tf_op jit(solution)/shard_map/all_gather | solution.py:42
  80.2 0.0 copy-start.1
  80.2 9.5 %fusion.10 = bf16[512,3,320]{0,2,1:T(8,128)(2,1)S(1)} fusion(bf16[512,5120]{1,0:T(8,128)(2,1)} %all-gather.4.cloned.1.call-done, bf16[3,5120,320]{1,2,0:T(8,128)(2,1)} %param.9, bf16[3,5120]{1,0:T(4,128)(2,1)S(1)} %bitcast.84), kind=kOutput, calls=%fused_computation.12 | convolution fusion | flops 5038571520 | bytes 16087040 | tf_op jit(solution)/shard_map/rd,cdh->rch/dot_general | solution.py:40
  89.7 0.0 copy-done.1
  89.7 0.0 copy-start.5
  89.7 0.0 copy-start
  89.7 0.6 fusion.23
  90.3 0.7 copy-done
  91.0 0.0 copy-start.2
  91.0 0.6 fusion.25
  91.6 0.4 copy-done.2
  92.0 0.6 fusion.27
  92.6 0.6 convolution_bitcast_fusion.1
  93.2 0.8 convolution_bitcast_fusion.2
  94.0 0.0 copy-done.5
  94.0 0.7 convolution_bitcast_fusion
  94.7 1.6 pad_maximum_fusion
  96.2 0.0 all-gather.6.cloned.1.call-update
  96.3 195.4 %all-gather.6.cloned.1.call-done = f32[48,320,640]{2,1,0:T(8,128)} async-done(((f32[3,320,640]{2,1,0:T(8,128)}), f32[48,320,640]{2,1,0:T(8,128)}) %all-gather.6.cloned.1.call-update) | async-done | bytes 39321616 | tf_op jit(solution)/shard_map/all_gather | solution.py:54
  291.6 13.9 %reduce_sum.36 = f32[3,320,640]{2,1,0:T(8,128)S(1)} reduce(f32[16,3,320,640]{3,2,1,0:T(8,128)} %bitcast.80, f32[]{:T(128)} %constant.3.clone.1), dimensions={0}, to_apply=%region_0.0 | reduce | flops 9216000 | bytes 41779204 | tf_op jit(solution)/shard_map/reduce_sum | solution.py:54
  305.6 0.0 copy-start.3
  305.6 1.6 fusion.4
  307.2 0.0 copy-done.3
  307.2 0.3 multiply_convert_fusion
  307.5 0.0 copy-start.4
  307.5 1.0 copy-done.4
  308.6 1.5 fusion.22
  310.1 2.3 multiply_reduce_fusion.1
  312.4 0.1 multiply_convert_fusion.6
  312.5 9.0 %all_to_all.19 = bf16[2,256,320]{1,2,0:T(8,128)(2,1)S(1)} all-to-all(bf16[2,256,320]{1,2,0:T(8,128)(2,1)S(1)} %bitcast.81), channel_id=1, replica_groups=mesh['seq'=16,'head'=2] {'head'}, dimensions={0} | all-to-all | bytes 655360 | tf_op jit(solution)/shard_map/all_to_all | solution.py:59
  321.5 0.9 copy.13
  (7 shorter events, 0.1 us)
Async XLA Ops:
  6.5 1.4 copy-start.7
  6.5 1.6 copy-start.6
  6.5 73.6 %all-gather.4.cloned.1.call-start = ((), (), s32[]{:S(2)}) async-start(), calls=%async_computation.1 | async-start | bytes 7864320 | tf_op jit(solution)/shard_map/all_gather | solution.py:42
  7.3 284.4 %all-gather.6.cloned.1.call-start = ((), (), s32[]{:S(2)}) async-start(), calls=%async_computation.2 | async-start | bytes 41779200 | tf_op jit(solution)/shard_map/all_gather | solution.py:54
  80.2 9.5 %copy-start.1 = (bf16[1,320,640]{2,1,0:T(8,128)(2,1)S(1)}, bf16[1,320,640]{2,1,0:T(8,128)(2,1)}, u32[]{:S(2)}) copy-start(bf16[1,320,640]{2,1,0:T(8,128)(2,1)} %param.13) | copy-start | bytes 1228804
  89.7 4.3 %copy-start.5 = (bf16[512,3,320]{0,2,1:T(8,128)(2,1)}, bf16[512,3,320]{0,2,1:T(8,128)(2,1)S(1)}, u32[]{:S(2)}) copy-start(bf16[512,3,320]{0,2,1:T(8,128)(2,1)S(1)} %fusion.10) | copy-start | bytes 2949124
  89.7 1.3 copy-start
  91.0 1.0 copy-start.2
  305.6 1.6 copy-start.3
  307.5 1.0 copy-start.4
Sparse Core Ops, SparseCore 0:
  8.9 71.2 all-gather.3
  96.4 195.1 all-gather.5
